TPU v7x, 32 devices: a whole 2x2x4 slice. The times are simulated.
32 devices in a mesh: expert: 8 (over z, x), hidden: 4 (over y, core).
Axes of the slice: x: 2, y: 2, z: 4, core: 2. Of those that a mesh axis runs over, the one named last changes fastest.
Arguments:
- tokens: bfloat16 [768, 4096], P('expert', 'hidden'), may hold values from -6 to 6
- gate_weight: bfloat16 [16, 4096, 1536], P('expert', None, 'hidden'), may hold values from -0.09375 to 0.09375
- up_weight: bfloat16 [16, 4096, 1536], P('expert', None, 'hidden'), may hold values from -0.09375 to 0.09375
- down_weight: bfloat16 [16, 1536, 4096], P('expert', 'hidden'), may hold values from -0.15625 to 0.15625
- swap_slot: int32 [8], replicated, may hold values from 0 to 1
- expert_ids: int32 [768, 8], P('expert'), may hold values from 0 to 15, as said below
- gate_fixed: int32 [768, 8], P('expert'), may hold values from 1 to 65535
Outputs:
- moe_out: bfloat16 [768, 4096], P('expert', 'hidden')
Inputs may be any that keep to these rules, and one draw needn't show every extreme that they name: `expert_ids`: each row names 8 ids on 8 different indices of the expert axis (index = id // 2). In the 96 rows of each index of the expert axis, every index is named exactly 96 times.
All inputs are finite; a program needn't handle non-finite values.
Results may differ from a plain program's by a relative error of at most 0.012.
Values may be sent and summed in bfloat16 or wider, within the bound.
A program may use at most 192 MiB of HBM per device.

v0:
```python
import jax
import jax.numpy as jnp
from jax import lax
from jax.sharding import PartitionSpec as P


def partner(value, axis, bit):
    return lax.ppermute(value, axis, [(i, i ^ 1 << bit) for i in range(lax.axis_size(axis))])


def per_device(tokens, gate_weight, up_weight, down_weight, swap_slot, expert_ids, gate_fixed):
    axis_count = lax.axis_size("expert")
    my_index = lax.axis_index("expert")
    tok_rows = tokens.shape[0]
    slots_here = gate_weight.shape[0]
    picks = expert_ids.shape[1]
    scores = gate_fixed.astype(jnp.float32)
    gate_norm = scores / jnp.sum(scores, axis=1, keepdims=True)
    target_dev = expert_ids // slots_here
    slot_local = expert_ids % slots_here
    capacity = picks * tok_rows // axis_count
    my_slot = swap_slot[my_index]
    top_bit = axis_count.bit_length() - 2
    traded = (
        lax.dynamic_index_in_dim(gate_weight, my_slot, 0, keepdims=False),
        lax.dynamic_index_in_dim(up_weight, my_slot, 0, keepdims=False),
        lax.dynamic_index_in_dim(down_weight, my_slot, 0, keepdims=False),
    )
    received = partner((traded[0], traded[1], traded[2]), "expert", top_bit)
    gate_set = lax.dynamic_update_index_in_dim(gate_weight, received[0], my_slot, 0)
    up_set = lax.dynamic_update_index_in_dim(up_weight, received[1], my_slot, 0)
    down_set = lax.dynamic_update_index_in_dim(down_weight, received[2], my_slot, 0)
    flat_target = target_dev.reshape(-1)
    one_hot = (flat_target[:, None] == jnp.arange(axis_count, dtype=jnp.int32)[None, :]).astype(
        jnp.int32
    )
    rank_count = jnp.cumsum(one_hot, axis=0) - one_hot
    rank_within = jnp.sum(rank_count * one_hot, axis=1)
    slot_index = flat_target * capacity + rank_within
    pair_count = flat_target.shape[0]
    source_row = (
        jnp.zeros((axis_count * capacity,), jnp.int32)
        .at[slot_index]
        .set(jnp.arange(pair_count, dtype=jnp.int32) // picks)
    )
    slot_tags = (
        jnp.full((axis_count * capacity,), -1, jnp.int32).at[slot_index].set(slot_local.reshape(-1))
    )
    send_tags = slot_tags.reshape(axis_count, capacity)
    gathered = lax.all_gather(tokens, "hidden", axis=1, tiled=True)
    send_rows = jnp.take(gathered, source_row, axis=0).reshape(
        axis_count, capacity, gathered.shape[1]
    )
    row_block = lax.all_to_all(send_rows, "expert", split_axis=0, concat_axis=0, tiled=True)
    width = row_block.shape[2]
    flat_rows = row_block.reshape(-1, width)
    flat_tags = lax.all_to_all(
        send_tags, "expert", split_axis=0, concat_axis=0, tiled=True
    ).reshape(-1)
    accum_rows = jnp.zeros((flat_rows.shape[0], down_set.shape[2]), jnp.float32)
    for slot_num in range(slots_here):
        gate_out = jnp.dot(flat_rows, gate_set[slot_num], preferred_element_type=jnp.float32)
        up_out = jnp.dot(flat_rows, up_set[slot_num], preferred_element_type=jnp.float32)
        hidden = jnp.where(
            flat_tags[:, None] == slot_num, jax.nn.silu(gate_out) * up_out, 0.0
        ).astype(jnp.bfloat16)
        accum_rows = accum_rows + jnp.dot(
            hidden, down_set[slot_num], preferred_element_type=jnp.float32
        )
    partial_value = accum_rows.reshape(row_block.shape[0], row_block.shape[1], -1)
    pair_slots = slot_index.reshape(tok_rows, picks)
    returned = lax.all_to_all(
        partial_value.astype(jnp.bfloat16), "expert", split_axis=0, concat_axis=0, tiled=True
    )
    flat_back = returned.reshape(axis_count * capacity, -1)
    combined = jnp.zeros((tok_rows, flat_back.shape[1]), jnp.float32)
    for pick in range(picks):
        combined = combined + gate_norm[:, pick : pick + 1] * jnp.take(
            flat_back, pair_slots[:, pick], axis=0
        ).astype(jnp.float32)
    result_rows = lax.psum_scatter(
        combined.astype(jnp.bfloat16), "hidden", scatter_dimension=1, tiled=True
    )
    return result_rows


def solution(mesh):
    in_specs = (
        P("expert", "hidden"),
        P("expert", None, "hidden"),
        P("expert", None, "hidden"),
        P("expert", "hidden", None),
        P(),
        P("expert", None),
        P("expert", None),
    )
    out_specs = P("expert", "hidden")
    return jax.shard_map(
        per_device, mesh=mesh, in_specs=in_specs, out_specs=out_specs, check_vma=False
    )
```

profile of v0, /device:TPU:8, one launch (start us, length us, event | category | flops | bytes accessed | tf_op | source)
XLA Modules:
  0.0 869.9 jit_solution(12613902266630627591)
XLA Ops:
  6.5 6.3 copy.34
  12.8 3.2 copy.35
  16.0 1.9 copy-done.1
  17.9 2.7 copy.36
  21.1 1.7 reduce-window.6
  22.8 0.1 copy.26
  23.0 0.2 reduce-window.9
  23.3 3.4 scatter_custom_fusion
  26.7 0.7 all_to_all.12
  27.4 6.3 all-to-all-start
  33.7 3.4 scatter_custom_fusion.1
  37.2 8.6 all_gather.3
  45.8 5.7 gather_fusion
  51.5 6.0 broadcast_select_fusion
  57.5 6.4 all-to-all-start.1
  63.9 0.6 dynamic_slice.14
  66.4 3.9 dynamic-slice_bitcast_fusion.2
  70.4 2.4 collective-permute-start
  72.7 3.8 dynamic-slice_bitcast_fusion.1
  76.6 0.6 collective-permute-start.1
  77.1 4.0 dynamic-slice_bitcast_fusion
  81.1 2.4 collective-permute-start.2
  83.7 386.0 %collective-permute-done = bf16[4096,384]{1,0:T(8,128)(2,1)} collective-permute-done((bf16[4096,384]{1,0:T(8,128)(2,1)}, bf16[4096,384]{1,0:T(8,128)(2,1)}, u32[]{:S(2)}, u32[]{:S(2)}) %collective-permute-start) | collective-permute-done | bytes 3145760 | tf_op jit(solution)/shard_map/ppermute | solution.py:8
  469.7 4.0 bitcast_dynamic-update-slice_fusion.2
  473.7 63.5 %collective-permute-done.1 = bf16[4096,384]{1,0:T(8,128)(2,1)S(1)} collective-permute-done((bf16[4096,384]{1,0:T(8,128)(2,1)}, bf16[4096,384]{1,0:T(8,128)(2,1)S(1)}, u32[]{:S(2)}, u32[]{:S(2)}) %collective-permute-start.1) | collective-permute-done | bytes 3145760 | tf_op jit(solution)/shard_map/ppermute | solution.py:8
  537.1 2.0 bitcast_dynamic-update-slice_fusion.1
  539.1 65.3 %collective-permute-done.2 = bf16[384,4096]{1,0:T(8,128)(2,1)} collective-permute-done((bf16[384,4096]{1,0:T(8,128)(2,1)}, bf16[384,4096]{1,0:T(8,128)(2,1)}, u32[]{:S(2)}, u32[]{:S(2)}) %collective-permute-start.2) | collective-permute-done | bytes 3145760 | tf_op jit(solution)/shard_map/ppermute | solution.py:8
  604.5 4.1 bitcast_dynamic-update-slice_fusion
  608.6 6.6 fusion.2
  615.2 5.6 fusion.4
  620.9 5.5 fusion.1
  626.4 5.5 fusion.3
  631.9 5.4 fusion
  637.3 7.6 add_convert_fusion
  644.9 7.2 all-to-all-start.2
  652.2 0.2 reduce-scatter.2.cloned.1.call-start
  652.5 0.4 slice_reduce_fusion.7
  653.1 134.4 %all-to-all-done.2 = bf16[8,96,4096]{2,1,0:T(8,128)(2,1)} async-done(((bf16[8,96,4096]{2,1,0:T(8,128)(2,1)}), bf16[8,96,4096]{2,1,0:T(8,128)(2,1)}, u32[]{:S(2)}, u32[]{:S(2)}) %all-to-all-start.2) | async-done | bytes 6291488 | tf_op jit(solution)/shard_map/all_to_all | solution.py:72
  787.5 5.4 gather_fusion.8
  792.9 5.4 gather_fusion.7
  798.3 5.4 gather_fusion.6
  803.7 5.4 gather_fusion.5
  809.1 6.4 gather_fusion.4
  815.4 6.5 gather_fusion.3
  821.9 6.3 gather_fusion.2
  828.2 6.3 gather_fusion.1
  834.5 4.6 add_convert_fusion.1
  839.1 23.5 %reduce-scatter.2.cloned.1.call-done = bf16[96,1024]{1,0:T(8,128)(2,1)} async-done(((bf16[96,4096]{1,0:T(8,128)(2,1)}), bf16[96,1024]{1,0:T(8,128)(2,1)}) %reduce-scatter.2.cloned.1.call-update) | async-done | bytes 196624 | tf_op jit(solution)/shard_map/reduce_scatter | solution.py:81
  (64 shorter events, 1.4 us)
Async XLA Ops:
  6.5 6.3 copy-start
  12.8 5.1 copy-start.1
  17.9 2.7 copy-start.4
  17.9 19.3 %copy-start.2 = (bf16[96,1024]{1,0:T(8,128)(2,1)S(1)}, bf16[96,1024]{1,0:T(8,128)(2,1)}, u32[]{:S(2)}) copy-start(bf16[96,1024]{1,0:T(8,128)(2,1)} %param.9) | copy-start | bytes 589828
  27.4 30.1 %all-to-all-start = ((s32[8,1,96]{2,1,0:T(1,128)}), s32[8,1,96]{2,1,0:T(1,128)S(1)}, u32[]{:S(2)}, u32[]{:S(2)}) async-start(s32[8,1,96]{2,1,0:T(1,128)} %all_to_all.12), calls=%async_computation | async-start | bytes 8192 | tf_op jit(solution)/shard_map/all_to_all | solution.py:57
  57.5 6.4 copy-start.5
  57.5 551.0 %all-to-all-start.1 = ((bf16[8,96,4096]{2,1,0:T(8,128)(2,1)}), bf16[8,96,4096]{2,1,0:T(8,128)(2,1)}, u32[]{:S(2)}, u32[]{:S(2)}) async-start(bf16[8,96,4096]{2,1,0:T(8,128)(2,1)} %broadcast_select_fusion), calls=%async_computation.1 | async-start | bytes 12582912 | tf_op jit(solution)/shard_map/all_to_all | solution.py:54
  70.4 399.4 %collective-permute-start = (bf16[4096,384]{1,0:T(8,128)(2,1)}, bf16[4096,384]{1,0:T(8,128)(2,1)}, u32[]{:S(2)}, u32[]{:S(2)}) collective-permute-start(bf16[4096,384]{1,0:T(8,128)(2,1)} %dynamic-slice_bitcast_fusion.2), channel_id=1, source_target_pairs={{0,16},{4,20},{8,24},{12,28},{16,0},{20,4},{24,8},{28,12},{1,17},{... | collective-permute-start | bytes 9437192 | tf_op jit(solution)/shard_map/ppermute | solution.py:8
  76.6 460.6 %collective-permute-start.1 = (bf16[4096,384]{1,0:T(8,128)(2,1)}, bf16[4096,384]{1,0:T(8,128)(2,1)S(1)}, u32[]{:S(2)}, u32[]{:S(2)}) collective-permute-start(bf16[4096,384]{1,0:T(8,128)(2,1)} %dynamic-slice_bitcast_fusion.1), channel_id=1, source_target_pairs={{0,16},{4,20},{8,24},{12,28},{16,0},{20,4},{24,8},{28,12},{1,17},{... | collective-permute-start | bytes 9437192 | tf_op jit(solution)/shard_map/ppermute | solution.py:8
  81.1 523.4 %collective-permute-start.2 = (bf16[384,4096]{1,0:T(8,128)(2,1)}, bf16[384,4096]{1,0:T(8,128)(2,1)}, u32[]{:S(2)}, u32[]{:S(2)}) collective-permute-start(bf16[384,4096]{1,0:T(8,128)(2,1)} %dynamic-slice_bitcast_fusion), channel_id=1, source_target_pairs={{0,16},{4,20},{8,24},{12,28},{16,0},{20,4},{24,8},{28,12},{1,17},{... | collective-permute-start | bytes 9437192 | tf_op jit(solution)/shard_map/ppermute | solution.py:8
  604.5 10.7 %slice-start.2 = ((s8[6291456]{0:T(1024)(128)(4,1)}), s8[2097152]{0:T(1024)(128)(4,1)S(1)}, s32[]{:S(2)}) async-start(s8[6291456]{0:T(1024)(128)(4,1)} %bitcast.71), calls=%async_computation.7 | async-start | bytes 4194304
  608.6 6.6 slice-start.3
  608.6 12.3 %slice-start = ((s8[6291456]{0:T(1024)(128)(4,1)}), s8[4194304]{0:T(1024)(128)(4,1)S(1)}, s32[]{:S(2)}) async-start(s8[6291456]{0:T(1024)(128)(4,1)} %bitcast.69), calls=%async_computation.5 | async-start | bytes 8388608
  615.2 5.7 slice-start.1
  644.9 8.1 copy-start.3
  644.9 142.6 %all-to-all-start.2 = ((bf16[8,96,4096]{2,1,0:T(8,128)(2,1)}), bf16[8,96,4096]{2,1,0:T(8,128)(2,1)}, u32[]{:S(2)}, u32[]{:S(2)}) async-start(bf16[8,96,4096]{2,1,0:T(8,128)(2,1)} %bitcast.67), calls=%async_computation.2 | async-start | bytes 12582912 | tf_op jit(solution)/shard_map/all_to_all | solution.py:72
  652.2 210.5 %reduce-scatter.2.cloned.1.call-start = ((), (), s32[]{:S(2)}) async-start(), calls=%async_computation.4 | async-start | bytes 983040 | tf_op jit(solution)/shard_map/reduce_scatter | solution.py:81
Sparse Core Ops, SparseCore 0:
  839.2 23.3 reduce-scatter.1
where the time goes:
time: 877 us; the launch traced here: 870 us
  waiting for transfers between devices  673 us (77%)
  local copies, waits for them, and re-layouts  97.9 us (11%)
  matrix products  36.2 us (4%)
  starting transfers between devices  25.3 us (3%)
  between operations  16.2 us (2%)
  other arithmetic  12.8 us (1%)
    ppermute x3, waiting for transfers between devices, partner(): lax.ppermute(value, axis, [(i, i ^ 1 << bit) for i in range(lax.axis_size...  515 us
    all_to_all x1, waiting for transfers between devices, per_device(): lax.all_to_all(partial_value.astype(jnp.bfloat16), 'expert', split_axis=0...  134 us
    gather x8, local copies, waits for them, and re-layouts, per_device(): jnp.take(flat_back, pair_slots[:, pick], axis=0).astype(jnp.float32)  47 us
    reduce_scatter x1, waiting for transfers between devices, per_device(): lax.psum_scatter(combined.astype(jnp.bfloat16), 'hidden', scatter_dimensi...  23.5 us
  transfers between devices with their start and end apart: 7, of which 5 were waited for; matrix products, arithmetic and copies ran while one was open for 4% of the time, Pallas kernels for 0%

commit v1 on v0

v1 whole, which is shorter than its diff:
```python
import jax
import jax.numpy as jnp
from jax import lax
from jax.sharding import PartitionSpec as P


def slot_weights(expert_ids, gate_fixed, swap_slot, slots_here):
    axis_count = lax.axis_size("expert")
    me = lax.axis_index("expert")
    scores = gate_fixed.astype(jnp.float32)
    gate_norm = scores / jnp.sum(scores, axis=1, keepdims=True)
    home = expert_ids // slots_here
    slot = expert_ids % slots_here
    onehot = home[:, :, None] == jnp.arange(axis_count, dtype=jnp.int32)
    own_swap = jnp.sum(jnp.where(onehot, swap_slot, 0), axis=2)
    other_swap = jnp.sum(jnp.where(onehot, jnp.roll(swap_slot, -(axis_count // 2)), 0), axis=2)
    other = (home + axis_count // 2) % axis_count
    source = jnp.where(slot == own_swap, other * slots_here + other_swap, expert_ids)
    mine = me * slots_here + jnp.arange(slots_here, dtype=jnp.int32)
    return jnp.sum(jnp.where(source[:, :, None] == mine, gate_norm[:, :, None], 0.0), axis=1)


def per_device(tokens, gate_weight, up_weight, down_weight, swap_slot, expert_ids, gate_fixed):
    slots_here = gate_weight.shape[0]
    ids_all = lax.all_gather(expert_ids, "expert", axis=0, tiled=True)
    gates_all = lax.all_gather(gate_fixed, "expert", axis=0, tiled=True)
    weight = slot_weights(ids_all, gates_all, swap_slot, slots_here)
    rows = lax.all_gather(tokens, "hidden", axis=1, tiled=True)
    rows = lax.all_gather(rows, "expert", axis=0, tiled=True)
    total = None
    for s in range(slots_here):
        gate_out = jnp.dot(rows, gate_weight[s], preferred_element_type=jnp.float32)
        up_out = jnp.dot(rows, up_weight[s], preferred_element_type=jnp.float32)
        hidden = (jax.nn.silu(gate_out) * up_out * weight[:, s : s + 1]).astype(jnp.bfloat16)
        out = jnp.dot(hidden, down_weight[s], preferred_element_type=jnp.float32)
        total = out if total is None else total + out
    total = total.astype(jnp.bfloat16)
    part = lax.psum_scatter(total, "expert", scatter_dimension=0, tiled=True)
    return lax.psum_scatter(part, "hidden", scatter_dimension=1, tiled=True)


def solution(mesh):
    in_specs = (
        P("expert", "hidden"),
        P("expert", None, "hidden"),
        P("expert", None, "hidden"),
        P("expert", "hidden", None),
        P(),
        P("expert", None),
        P("expert", None),
    )
    return jax.shard_map(
        per_device, mesh=mesh, in_specs=in_specs, out_specs=P("expert", "hidden"), check_vma=False
    )
```

time: 877 us -> 302 us (0.34)
  waiting for transfers between devices: 673 us -> 179 us
  local copies, waits for them, and re-layouts: 97.9 us -> 1.11 us
  blocking collectives: 8.61 us -> 69.7 us
  starting transfers between devices: 25.3 us -> 0.09 us
  other arithmetic: 12.8 us -> 1.11 us
    ppermute x3 -> x0, waiting for transfers between devices: 515 us -> none  [partner(): lax.ppermute(value, axis, [(i, i ^ 1 << bit) for i in range(lax.axis_size...]
    all_to_all x3 -> x0, waiting for transfers between devices: 134 us -> none  [the longest x1 134 us: per_device(): lax.all_to_all(partial_value.astype(jnp.bfloat16), 'expert', split_axis=0...]
    reduce_scatter x1 -> x2, waiting for transfers between devices: 23.5 us -> 143 us  [the longest x1 117 us: per_device(): part = lax.psum_scatter(total, 'expert', scatter_dimension=0, tiled=True)]
    all_gather x1 -> x3, blocking collectives: 8.61 us -> 69.7 us  [the longest x1 31.1 us: per_device(): ids_all = lax.all_gather(expert_ids, 'expert', axis=0, tiled=True)]
    gather x9 -> x0, local copies, waits for them, and re-layouts: 52.7 us -> none  [the longest x8 47 us: per_device(): jnp.take(flat_back, pair_slots[:, pick], axis=0).astype(jnp.float32)]
    all_gather x0 -> x1, waiting for transfers between devices: none -> 36.8 us  [per_device(): rows = lax.all_gather(rows, 'expert', axis=0, tiled=True)]
    all_to_all x3 -> x0, starting transfers between devices: 19.9 us -> none  [the longest x1 7.25 us: per_device(): lax.all_to_all(partial_value.astype(jnp.bfloat16), 'expert', split_axis=0...]
    unnamed x24 -> x15, local copies, waits for them, and re-layouts: 14.1 us -> 0.12 us
  transfers between devices with their start and end apart: 7 -> 3, of which waited for: 5 -> 3; matrix products, arithmetic and copies ran while one was open for 4% -> 1% of each run, Pallas kernels for 0% -> 0%
where the time goes in v1:
time: 302 us; the launch traced here: 300 us
  waiting for transfers between devices  179 us (59%)
  blocking collectives  69.7 us (23%)
  matrix products  35.1 us (12%)
  between operations  13.3 us (4%)
    reduce_scatter x1, waiting for transfers between devices, per_device(): part = lax.psum_scatter(total, 'expert', scatter_dimension=0, tiled=True)  117 us
    all_gather x1, waiting for transfers between devices, per_device(): rows = lax.all_gather(rows, 'expert', axis=0, tiled=True)  36.8 us
    all_gather x1, blocking collectives, per_device(): ids_all = lax.all_gather(expert_ids, 'expert', axis=0, tiled=True)  31.1 us
    all_gather x1, blocking collectives, per_device(): gates_all = lax.all_gather(gate_fixed, 'expert', axis=0, tiled=True)  28.4 us
    reduce_scatter x1, waiting for transfers between devices, per_device(): return lax.psum_scatter(part, 'hidden', scatter_dimension=1, tiled=True)  25.7 us
    dot_general x2, matrix products, per_device(): gate_out = jnp.dot(rows, gate_weight[s], preferred_element_type=jnp.float32)  12.2 us
    dot_general x2, matrix products, per_device(): up_out = jnp.dot(rows, up_weight[s], preferred_element_type=jnp.float32)  12.1 us
    dot_general x2, matrix products, per_device(): out = jnp.dot(hidden, down_weight[s], preferred_element_type=jnp.float32)  10.8 us
  transfers between devices with their start and end apart: 3, of which 3 were waited for; matrix products, arithmetic and copies ran while one was open for 1% of the time, Pallas kernels for 0%

profile of v1, /device:TPU:8, one launch (start us, length us, event | category | flops | bytes accessed | tf_op | source)
XLA Modules:
  0.0 299.8 jit_solution(4140914008804489191)
XLA Ops:
  6.5 0.0 all-gather.4.cloned.1.call-start
  6.5 10.3 %all_gather.12 = bf16[96,4096]{1,0:T(8,128)(2,1)} all-gather(bf16[96,1024]{1,0:T(8,128)(2,1)} %param.7), channel_id=1, replica_groups=mesh['expert'=8,'hidden'=4] {'hidden'}, dimensions={1}, use_global_device_ids=true | all-gather | bytes 983040 | tf_op jit(solution)/shard_map/all_gather | solution.py:28
  16.8 0.0 all-gather.4.cloned.1.call-update
  16.8 0.0 reduce-scatter.3.cloned.1.call-start
  16.9 28.4 %all-gather.1 = s32[8,96,8]{1,2,0:T(8,128)S(1)} all-gather(s32[1,96,8]{1,2,0:T(8,128)} %bitcast.44), channel_id=1, replica_groups=mesh['expert'=8,'hidden'=4] {'expert'}, dimensions={0}, use_global_device_ids=true | all-gather | bytes 27648 | tf_op jit(solution)/shard_map/all_gather | solution.py:26
  45.3 0.1 reshape.12
  45.4 0.1 reshape.13
  45.4 31.1 %all-gather = s32[8,96,8]{1,2,0:T(8,128)S(1)} all-gather(s32[1,96,8]{1,2,0:T(8,128)} %bitcast.45), channel_id=1, replica_groups=mesh['expert'=8,'hidden'=4] {'expert'}, dimensions={0}, use_global_device_ids=true | all-gather | bytes 27648 | tf_op jit(solution)/shard_map/all_gather | solution.py:25
  76.5 0.1 reshape.9
  76.6 0.8 fusion.42
  77.4 0.1 pad_add_fusion
  77.5 0.8 select_reduce_fusion.1
  78.4 0.1 select_reduce_fusion.2
  78.5 36.8 %all-gather.4.cloned.1.call-done = bf16[768,4096]{1,0:T(8,128)(2,1)} async-done(((bf16[96,4096]{1,0:T(8,128)(2,1)}), bf16[768,4096]{1,0:T(8,128)(2,1)}) %all-gather.4.cloned.1.call-update) | async-done | bytes 6291472 | tf_op jit(solution)/shard_map/all_gather | solution.py:29
  115.3 0.0 copy-start
  115.3 0.0 slice-start
  115.3 0.0 slice-start.2
  115.3 6.6 %fusion.9 = f32[768,384]{1,0:T(8,128)S(1)} fusion(bf16[768,4096]{1,0:T(8,128)(2,1)} %all-gather.4.cloned.1.call-done, bf16[2,4096,384]{2,1,0:T(8,128)(2,1)} %param.8), kind=kOutput, calls=%fused_computation.10 | convolution fusion | flops 2415919104 | bytes 10616832 | tf_op jit(solution)/shard_map/dot_general | solution.py:32
  121.9 0.0 copy-done
  121.9 0.0 slice-start.1
  121.9 0.0 slice-start.3
  121.9 5.8 %fusion.29 = bf16[768,384]{1,0:T(8,128)(2,1)S(1)} fusion(bf16[768,4096]{1,0:T(8,128)(2,1)S(1)} %copy-done, bf16[2,4096,384]{2,1,0:T(8,128)(2,1)} %param.9, f32[768,384]{1,0:T(8,128)S(1)} %fusion.9, f32[768]{0:T(1024)S(1)} %get-tuple-element.8), kind=kOutput, calls=%fused_computation.22 | convolution fusion | flops 2417983488 | bytes 11209728 | tf_op jit(solution)/shard_map/dot_general | solution.py:33
  127.7 0.0 slice-done
  127.7 0.0 slice-done.1
  127.7 0.0 slice-start.4
  127.7 3.4 %fusion.5 = f32[768,4096]{1,0:T(8,128)S(1)} fusion(bf16[768,384]{1,0:T(8,128)(2,1)S(1)} %fusion.29, bf16[2,384,4096]{2,1,0:T(8,128)(2,1)S(1)} %bitcast.43), kind=kOutput, calls=%fused_computation.6 | convolution fusion | flops 2415919104 | bytes 16318464 | tf_op jit(solution)/shard_map/dot_general | solution.py:35
  131.2 0.0 slice-done.2
  131.2 0.0 slice-done.3
  131.2 0.0 slice-start.5
  131.2 5.7 %fusion.3 = f32[768,384]{1,0:T(8,128)S(1)} fusion(bf16[768,4096]{1,0:T(8,128)(2,1)} %all-gather.4.cloned.1.call-done, bf16[2,4096,384]{2,1,0:T(8,128)(2,1)S(1)} %bitcast.47), kind=kOutput, calls=%fused_computation.4 | convolution fusion | flops 2415919104 | bytes 10616832 | tf_op jit(solution)/shard_map/dot_general | solution.py:32
  136.9 0.0 slice-done.4
  136.9 0.0 slice-done.5
  136.9 6.3 %fusion.32 = bf16[768,384]{1,0:T(8,128)(2,1)S(1)} fusion(bf16[768,4096]{1,0:T(8,128)(2,1)} %all-gather.4.cloned.1.call-done, bf16[2,4096,384]{2,1,0:T(8,128)(2,1)S(1)} %bitcast.49, f32[768,384]{1,0:T(8,128)S(1)} %fusion.3, f32[768]{0:T(1024)S(1)} %get-tuple-element.7), kind=kOutput, calls=%fused_computation.23 | convolution fusion | flops 2417983488 | bytes 11210752 | tf_op jit(solution)/shard_map/dot_general | solution.py:33
  143.2 7.3 %add_convert_fusion = bf16[768,4096]{1,0:T(8,128)(2,1)} fusion(f32[768,4096]{1,0:T(8,128)S(1)} %fusion.5, bf16[768,384]{1,0:T(8,128)(2,1)S(1)} %fusion.32, bf16[2,384,4096]{2,1,0:T(8,128)(2,1)} %param.10), kind=kOutput, calls=%fused_computation | convolution fusion | flops 2422210560 | bytes 22609920 | tf_op jit(solution)/shard_map/dot_general | solution.py:35
  150.6 0.0 reduce-scatter.3.cloned.1.call-update
  150.6 0.0 reduce-scatter.5.cloned.1.call-start
  150.6 117.0 %reduce-scatter.3.cloned.1.call-done = bf16[96,4096]{1,0:T(8,128)(2,1)} async-done(((bf16[768,4096]{1,0:T(8,128)(2,1)}), bf16[96,4096]{1,0:T(8,128)(2,1)}) %reduce-scatter.3.cloned.1.call-update) | async-done | bytes 786448 | tf_op jit(solution)/shard_map/reduce_scatter | solution.py:38
  267.6 0.0 reduce-scatter.5.cloned.1.call-update
  267.6 25.7 %reduce-scatter.5.cloned.1.call-done = bf16[96,1024]{1,0:T(8,128)(2,1)} async-done(((bf16[96,4096]{1,0:T(8,128)(2,1)}), bf16[96,1024]{1,0:T(8,128)(2,1)}) %reduce-scatter.5.cloned.1.call-update) | async-done | bytes 196624 | tf_op jit(solution)/shard_map/reduce_scatter | solution.py:39
  (12 shorter events, 0.1 us)
Async XLA Ops:
  6.5 108.7 %all-gather.4.cloned.1.call-start = ((), (), s32[]{:S(2)}) async-start(), calls=%async_computation.2 | async-start | bytes 7077888 | tf_op jit(solution)/shard_map/all_gather | solution.py:29
  16.8 250.8 %reduce-scatter.3.cloned.1.call-start = ((), (), s32[]{:S(2)}) async-start(), calls=%async_computation.3 | async-start | bytes 7077888 | tf_op jit(solution)/shard_map/reduce_scatter | solution.py:38
  115.3 6.6 %copy-start = (bf16[768,4096]{1,0:T(8,128)(2,1)S(1)}, bf16[768,4096]{1,0:T(8,128)(2,1)}, u32[]{:S(2)}) copy-start(bf16[768,4096]{1,0:T(8,128)(2,1)} %all-gather.4.cloned.1.call-done) | copy-start | bytes 18874372
  115.3 12.4 %slice-start = ((s8[6291456]{0:T(1024)(128)(4,1)}), s8[4194304]{0:T(1024)(128)(4,1)S(1)}, s32[]{:S(2)}) async-start(s8[6291456]{0:T(1024)(128)(4,1)} %bitcast.42), calls=%async_computation.5 | async-start | bytes 8388608
  115.3 15.9 %slice-start.2 = ((s8[6291456]{0:T(1024)(128)(4,1)}), s8[4194304]{0:T(1024)(128)(4,1)S(1)}, s32[]{:S(2)}) async-start(s8[6291456]{0:T(1024)(128)(4,1)} %bitcast.46), calls=%async_computation.7 | async-start | bytes 8388608
  121.9 5.8 %slice-start.1 = ((s8[6291456]{0:T(1024)(128)(4,1)}), s8[2097152]{0:T(1024)(128)(4,1)S(1)}, s32[]{:S(2)}) async-start(s8[6291456]{0:T(1024)(128)(4,1)} %bitcast.42), calls=%async_computation.6 | async-start | bytes 4194304
  121.9 9.3 %slice-start.3 = ((s8[6291456]{0:T(1024)(128)(4,1)}), s8[2097152]{0:T(1024)(128)(4,1)S(1)}, s32[]{:S(2)}) async-start(s8[6291456]{0:T(1024)(128)(4,1)} %bitcast.46), calls=%async_computation.8 | async-start | bytes 4194304
  127.7 9.2 %slice-start.4 = ((s8[6291456]{0:T(1024)(128)(4,1)}), s8[2097152]{0:T(1024)(128)(4,1)S(1)}, s32[]{:S(2)}) async-start(s8[6291456]{0:T(1024)(128)(4,1)} %bitcast.48), calls=%async_computation.9 | async-start | bytes 4194304
  131.2 5.7 %slice-start.5 = ((s8[6291456]{0:T(1024)(128)(4,1)}), s8[4194304]{0:T(1024)(128)(4,1)S(1)}, s32[]{:S(2)}) async-start(s8[6291456]{0:T(1024)(128)(4,1)} %bitcast.48), calls=%async_computation.10 | async-start | bytes 8388608
  150.6 142.7 %reduce-scatter.5.cloned.1.call-start = ((), (), s32[]{:S(2)}) async-start(), calls=%async_computation.4 | async-start | bytes 983040 | tf_op jit(solution)/shard_map/reduce_scatter | solution.py:39
Sparse Core Ops, SparseCore 0:
  16.9 98.2 all-gather.3
  150.7 116.8 reduce-scatter.2
  270.1 23.1 reduce-scatter.4

commit v2 on v1

--- a/solution.py
+++ b/solution.py
@@ -1,7 +1,13 @@
 import jax
 import jax.numpy as jnp
 from jax import lax
+from jax.experimental import pallas as pl
+from jax.experimental.pallas import tpu as pltpu
 from jax.sharding import PartitionSpec as P
+
+MESH = pl.DeviceIdType.MESH
+F32 = jnp.float32
+BF16 = jnp.bfloat16
 
 
 def slot_weights(expert_ids, gate_fixed, swap_slot, slots_here):
@@ -20,7 +26,7 @@
     return jnp.sum(jnp.where(source[:, :, None] == mine, gate_norm[:, :, None], 0.0), axis=1)
 
 
-def per_device(tokens, gate_weight, up_weight, down_weight, swap_slot, expert_ids, gate_fixed):
+def dense_device(tokens, gate_weight, up_weight, down_weight, swap_slot, expert_ids, gate_fixed):
     slots_here = gate_weight.shape[0]
     ids_all = lax.all_gather(expert_ids, "expert", axis=0, tiled=True)
     gates_all = lax.all_gather(gate_fixed, "expert", axis=0, tiled=True)
@@ -39,6 +45,295 @@
     return lax.psum_scatter(part, "hidden", scatter_dimension=1, tiled=True)
 
 
+def fused_kernel(
+    tok_ref, gate_ref, up_ref, down_ref, ids_ref, fix_ref, swap_ref, out_ref,
+    buf, wgu, wd, hid, wcol, pbuf, wt, rs_sib, rs_sec, rs_fst, rs_z, own_sum,
+    load_sem, ag_send, ag_recv, wt_send, wt_recv, rs_send, rs_recv,
+):
+    rows, cols = tok_ref.shape
+    slots, width, ff = gate_ref.shape
+    tiles = ff // 128
+    e, h = lax.axis_index("expert"), lax.axis_index("hidden")
+    z, x = lax.div(e, 2), lax.rem(e, 2)
+    y, c = lax.div(h, 2), lax.rem(h, 2)
+    zs = [z, z + 1 - 2 * lax.rem(z, 2), lax.rem(z + 2, 4), 3 - z]
+    fx, fy = x + (1 - c) * (1 - 2 * x), y + c * (1 - 2 * y)
+    sx, sy = x + c * (1 - 2 * x), y + (1 - c) * (1 - 2 * y)
+
+    def dev(zz, xx, yy, cc):
+        return (zz * 2 + xx, yy * 2 + cc)
+
+    line = [dev(zs[k], x, y, c) for k in range(4)]
+    cross = [dev(zs[k], 1 - x, y, c) for k in range(4)]
+    first, second, sibling = dev(z, fx, fy, c), dev(z, sx, sy, c), dev(z, x, y, 1 - c)
+
+    loads = []
+
+    def load(source, target):
+        copy = pltpu.make_async_copy(source, target, load_sem.at[len(loads)])
+        copy.start()
+        loads.append(copy)
+
+    def row_slice(xx):
+        return pl.ds(pl.multiple_of(xx * rows, 32), rows)
+
+    def block(k, yy, xx, cc):
+        return buf.at[k, yy * 2 + cc, row_slice(xx), :]
+
+    load(tok_ref, block(0, y, x, c))
+    for s in range(slots):
+        for j in range(tiles):
+            span = pl.ds(j * 128, 128)
+            load(gate_ref.at[s, :, span], wgu.at[s * tiles + j, :, pl.ds(0, 128)])
+            load(up_ref.at[s, :, span], wgu.at[s * tiles + j, :, pl.ds(128, 128)])
+    for s in range(slots):
+        load(down_ref.at[s], wd.at[pl.ds(s * ff, ff), :])
+
+    ids = ids_ref[...]
+    scores = fix_ref[...].astype(F32)
+    gate_norm = scores / jnp.sum(scores, axis=1, keepdims=True)
+    axis_count = swap_ref.shape[0]
+    home = lax.div(ids, slots)
+    own_swap = jnp.zeros_like(ids)
+    other_swap = jnp.zeros_like(ids)
+    for j in range(axis_count):
+        own_swap = jnp.where(home == j, swap_ref[j], own_swap)
+        other_swap = jnp.where(home == j, swap_ref[(j + axis_count // 2) % axis_count], other_swap)
+    other = lax.rem(home + axis_count // 2, axis_count)
+    source = jnp.where(ids - home * slots == own_swap, other * slots + other_swap, ids)
+    lane = lax.broadcasted_iota(jnp.int32, (rows, 128), 1)
+    table = jnp.zeros((rows, 128), F32)
+    for k in range(ids.shape[1]):
+        table = table + jnp.where(source[:, k : k + 1] == lane, gate_norm[:, k : k + 1], 0.0)
+    table = jnp.concatenate([table, jnp.zeros((128 - rows, 128), F32)], axis=0)
+    wt[0, x] = jnp.transpose(table)[: wt.shape[2]]
+
+    barrier = pltpu.get_barrier_semaphore()
+    peers = line[1:] + cross[1:] + [first, second, sibling]
+    for peer in peers:
+        pl.semaphore_signal(barrier, inc=1, device_id=peer, device_id_type=MESH)
+    pl.semaphore_wait(barrier, len(peers))
+
+    started = []
+
+    def remote(source, target, sends, recvs, i, peer):
+        return pltpu.make_async_remote_copy(
+            src_ref=source, dst_ref=target, send_sem=sends.at[i], recv_sem=recvs.at[i],
+            device_id=peer, device_id_type=MESH,
+        )
+
+    def send(*what):
+        copy = remote(*what)
+        copy.start()
+        started.append(copy)
+
+    def gather(i, source, target, peer):
+        send(source, target, ag_send, ag_recv, i, peer)
+
+    def arrived(i, target, peer):
+        remote(target, target, ag_send, ag_recv, i, peer).wait_recv()
+
+    def base(k):
+        return 3 + 7 * k
+
+    def a0(k):
+        if k > 3:
+            return
+        mine = block(k, y, x, c)
+        if k:
+            arrived(k - 1, mine, line[k])
+        gather(base(k), mine, mine, first)
+        gather(base(k) + 1, mine, mine, second)
+        gather(base(k) + 3, mine, mine, sibling)
+
+    def a1(k):
+        if k > 3:
+            return
+        got = block(k, fy, fx, c)
+        arrived(base(k), got, first)
+        gather(base(k) + 2, got, got, second)
+        gather(base(k) + 4, got, got, sibling)
+
+    def a2(k):
+        if k > 3:
+            return
+        for n, got in enumerate([block(k, sy, sx, c), block(k, 1 - y, 1 - x, c)]):
+            arrived(base(k) + 1 + n, got, second)
+            gather(base(k) + 5 + n, got, got, sibling)
+
+    def a3(k):
+        if k > 3:
+            return
+        for n, (yy, xx) in enumerate([(y, x), (sy, sx), (fy, fx), (1 - y, 1 - x)]):
+            arrived(base(k) + 3 + n, block(k, yy, xx, 1 - c), sibling)
+
+    a_me, b_me = y + c * (x - y), x + c * (y - x)
+
+    def scatter(i, source, target, peer):
+        send(source, target, rs_send, rs_recv, i, peer)
+
+    def summed(i, target, peer):
+        remote(target, target, rs_send, rs_recv, i, peer).wait_recv()
+
+    def r0(k):
+        scatter(4 * k, pbuf.at[k, 1 - c], rs_sib.at[k], sibling)
+
+    def r1(k):
+        if k < 0:
+            return
+        summed(4 * k, rs_sib.at[k], sibling)
+        away = 1 - a_me
+        pbuf[k, c, away] = (pbuf[k, c, away].astype(F32) + rs_sib[k, away].astype(F32)).astype(BF16)
+        scatter(4 * k + 1, pbuf.at[k, c, away], rs_sec.at[k], second)
+        pbuf[k, c, a_me] = (pbuf[k, c, a_me].astype(F32) + rs_sib[k, a_me].astype(F32)).astype(BF16)
+
+    def r2(k):
+        if k < 0:
+            return
+        summed(4 * k + 1, rs_sec.at[k], second)
+        away = 1 - b_me
+        pbuf[k, c, a_me, away] = (
+            pbuf[k, c, a_me, away].astype(F32) + rs_sec[k, away].astype(F32)
+        ).astype(BF16)
+        scatter(4 * k + 2, pbuf.at[k, c, a_me, away], rs_fst.at[k], first)
+
+    def r3(k):
+        if k < 0:
+            return
+        summed(4 * k + 2, rs_fst.at[k], first)
+        total = (
+            pbuf[k, c, a_me, b_me].astype(F32)
+            + rs_sec[k, b_me].astype(F32)
+            + rs_fst[k].astype(F32)
+        )
+        if k:
+            pbuf[k, c, a_me, b_me] = total.astype(BF16)
+            scatter(4 * k + 3, pbuf.at[k, c, a_me, b_me], rs_z.at[k - 1], line[k])
+        else:
+            own_sum[...] = total
+
+    def weight_columns(k):
+        for xx in range(2):
+            part = wt[k, xx]
+            sub = lax.broadcasted_iota(jnp.int32, part.shape, 0)
+            for s in range(slots):
+                row = jnp.sum(jnp.where(sub == e * slots + s, part, 0.0), axis=0, keepdims=True)
+                column = jnp.transpose(jnp.broadcast_to(row, (128, 128)))
+                wcol[s, xx * rows : (xx + 1) * rows, :] = column[:rows]
+
+    def up_gate(k, s):
+        @pl.loop(0, tiles)
+        def _(j):
+            acc = jnp.zeros((2 * rows, 256), F32)
+            for q in range(buf.shape[1]):
+                acc = acc + jnp.dot(
+                    buf[k, q], wgu[s * tiles + j, q * cols : (q + 1) * cols, :],
+                    preferred_element_type=F32,
+                )
+            gate_out, up_out = acc[:, :128], acc[:, 128:]
+            value = gate_out / (1.0 + jnp.exp(-gate_out)) * up_out * wcol[s]
+            hid[:, pl.ds(pl.multiple_of(s * ff + j * 128, 128), 128)] = value.astype(BF16)
+
+    def down(k):
+        for q in range(buf.shape[1]):
+            out = jnp.dot(hid[...], wd[:, q * cols : (q + 1) * cols], preferred_element_type=F32)
+            out = out.astype(BF16)
+            yy, cc = q // 2, q % 2
+            for xx in range(2):
+                a, b = (yy, xx) if cc == 0 else (xx, yy)
+                pbuf[k, cc, a, b] = out[xx * rows : (xx + 1) * rows]
+
+    loads[0].wait()
+    gather_own = block(0, y, x, c)
+    a0(0)
+    for k in (1, 2, 3):
+        gather(k - 1, gather_own, block(k, y, x, c), line[k])
+    tags = [(line[1], 1, 0), (line[2], 2, 1), (line[3], 3, 2)]
+    tags += [(cross[k], k, 3 + k) for k in range(4)]
+    for peer, k, i in tags:
+        send(wt.at[0, x], wt.at[k, x], wt_send, wt_recv, i, peer)
+    a1(0)
+    a0(1)
+    a2(0)
+    a1(1)
+    for peer, k, i in tags:
+        got = wt.at[k, x if i < 3 else 1 - x]
+        remote(got, got, wt_send, wt_recv, i, peer).wait_recv()
+    a0(2)
+    for copy in loads[1:]:
+        copy.wait()
+    a3(0)
+    for k in range(4):
+        weight_columns(k)
+        up_gate(k, 0)
+        a2(k + 1)
+        a1(k + 2)
+        r1(k - 1)
+        up_gate(k, 1)
+        a0(k + 3)
+        r2(k - 1)
+        down(k)
+        r0(k)
+        r3(k - 1)
+        a3(k + 1)
+    r1(3)
+    r2(3)
+    r3(3)
+    total = own_sum[...]
+    for k in (1, 2, 3):
+        summed(4 * k + 3, rs_z.at[k - 1], line[k])
+        total = total + rs_z[k - 1].astype(F32)
+    out_ref[...] = total.astype(BF16)
+    for copy in started:
+        copy.wait_send()
+
+
+def fused_device(tokens, gate_weight, up_weight, down_weight, swap_slot, expert_ids, gate_fixed):
+    rows, cols = tokens.shape
+    slots, width, ff = gate_weight.shape
+    quarters = width // cols
+    chunks = 4
+    scratch = [
+        pltpu.VMEM((chunks, quarters, 2 * rows, cols), BF16),
+        pltpu.VMEM((slots * ff // 128, width, 256), BF16),
+        pltpu.VMEM((slots * ff, width), BF16),
+        pltpu.VMEM((2 * rows, slots * ff), BF16),
+        pltpu.VMEM((slots, 2 * rows, 128), F32),
+        pltpu.VMEM((chunks, 2, 2, 2, rows, cols), BF16),
+        pltpu.VMEM((chunks, 2, 16, 128), F32),
+        pltpu.VMEM((chunks, 2, 2, rows, cols), BF16),
+        pltpu.VMEM((chunks, 2, rows, cols), BF16),
+        pltpu.VMEM((chunks, rows, cols), BF16),
+        pltpu.VMEM((chunks - 1, rows, cols), BF16),
+        pltpu.VMEM((rows, cols), F32),
+        pltpu.SemaphoreType.DMA((1 + 2 * slots * (ff // 128) + slots,)),
+        pltpu.SemaphoreType.DMA((3 + 7 * chunks,)),
+        pltpu.SemaphoreType.DMA((3 + 7 * chunks,)),
+        pltpu.SemaphoreType.DMA((7,)),
+        pltpu.SemaphoreType.DMA((7,)),
+        pltpu.SemaphoreType.DMA((4 * chunks,)),
+        pltpu.SemaphoreType.DMA((4 * chunks,)),
+    ]
+    any_space = pl.BlockSpec(memory_space=pl.ANY)
+    vmem = pl.BlockSpec(memory_space=pltpu.VMEM)
+    return pl.pallas_call(
+        fused_kernel,
+        out_shape=jax.ShapeDtypeStruct((rows, cols), BF16),
+        in_specs=[any_space] * 4 + [vmem, vmem, pl.BlockSpec(memory_space=pltpu.SMEM)],
+        out_specs=vmem,
+        scratch_shapes=scratch,
+        compiler_params=pltpu.CompilerParams(
+            collective_id=0, has_side_effects=True, vmem_limit_bytes=56 * 1024 * 1024
+        ),
+    )(tokens, gate_weight, up_weight, down_weight, expert_ids, gate_fixed, swap_slot)
+
+
+def per_device(tokens, *rest):
+    small = lax.axis_size("expert") == 8 and lax.axis_size("hidden") == 4
+    fits = tokens.shape == (96, 1024) and rest[0].shape == (2, 4096, 384)
+    return fused_device(tokens, *rest) if small and fits else dense_device(tokens, *rest)
+
+
 def solution(mesh):
     in_specs = (
         P("expert", "hidden"),

time: 302 us -> 110 us (0.36)
  waiting for transfers between devices: 179 us -> 0 us
  Pallas kernels: 0 us -> 105 us
  blocking collectives: 69.7 us -> 0 us
  matrix products: 35.1 us -> 0 us
  between operations: 13.3 us -> 0.01 us
  local copies, waits for them, and re-layouts: 1.11 us -> 4.41 us
    reduce_scatter x2 -> x0, waiting for transfers between devices: 143 us -> none  [the longest x1 117 us: per_device(): part = lax.psum_scatter(total, 'expert', scatter_dimension=0, tiled=True)]
    pallas_call x0 -> x1, Pallas kernels: none -> 105 us  [fused_device(): pl.pallas_call(fused_kernel, out_shape=jax.ShapeDtypeStruct((rows, cols),...]
    all_gather x3 -> x0, blocking collectives: 69.7 us -> none  [the longest x1 31.1 us: per_device(): ids_all = lax.all_gather(expert_ids, 'expert', axis=0, tiled=True)]
    all_gather x1 -> x0, waiting for transfers between devices: 36.8 us -> none  [per_device(): rows = lax.all_gather(rows, 'expert', axis=0, tiled=True)]
    dot_general x6 -> x0, matrix products: 35.1 us -> none  [the longest x2 12.2 us: per_device(): gate_out = jnp.dot(rows, gate_weight[s], preferred_element_type=jnp.float32)]
    unnamed x15 -> x3, local copies, waits for them, and re-layouts: 0.12 us -> 4.41 us
  transfers between devices with their start and end apart: 3 -> 0, of which waited for: 3 -> 0; matrix products, arithmetic and copies ran while one was open for 1% -> 0% of each run, Pallas kernels for 0% -> 0%
where the time goes in v2:
time: 110 us; the launch traced here: 109 us
  Pallas kernels  105 us (95%)
  local copies, waits for them, and re-layouts  4.41 us (4%)
    pallas_call x1, Pallas kernels, fused_device(): pl.pallas_call(fused_kernel, out_shape=jax.ShapeDtypeStruct((rows, cols),...  105 us
    unnamed x3, local copies, waits for them, and re-layouts  4.41 us

profile of v2, /device:TPU:8, one launch (start us, length us, event | category | flops | bytes accessed | tf_op | source)
XLA Modules:
  0.0 109.3 jit_solution(6574349936383928041)
XLA Ops:
  0.0 1.4 %copy.8.ids_ref = s32[96,8]{1,0:T(8,128)} copy(s32[96,8]{0,1:T(8,128)} %param.12) | data formatting | bytes 6144 | tf_op args[5]
  1.4 1.4 %copy.9.fix_ref = s32[96,8]{1,0:T(8,128)} copy(s32[96,8]{0,1:T(8,128)} %param.13) | data formatting | bytes 6144 | tf_op args[6]
  2.8 104.9 %shard_map.73 = bf16[96,1024]{1,0:T(8,128)(2,1)} custom-call(bf16[96,1024]{1,0:T(8,128)(2,1)} %tok_ref.1, bf16[2,4096,384]{2,1,0:T(8,128)(2,1)} %gate_ref.1, bf16[2,4096,384]{2,1,0:T(8,128)(2,1)} %up_ref.1, bf16[2,384,4096]{2,1,0:T(8,128)(2,1)} %down_ref.1, s32[96,8]{1,0:T(8,128)} %copy.8.ids_ref, s32[96,8]{1,0:T(8,128)} %copy.9.fix_ref, s32[8]{0:T(128)} %swap_ref.1), custom_call_target="tpu_custom_call" | custom-call | tf_op jit(solution)/shard_map/pallas_call | solution.py:319
  107.7 1.6 %copy.11 = bf16[96,1024]{1,0:T(8,128)(2,1)} copy(bf16[96,1024]{1,0:T(8,128)(2,1)} %shard_map.73) | data formatting | bytes 393216

commit v3 on v2

--- a/solution.py
+++ b/solution.py
@@ -57,15 +57,18 @@
     z, x = lax.div(e, 2), lax.rem(e, 2)
     y, c = lax.div(h, 2), lax.rem(h, 2)
     zs = [z, z + 1 - 2 * lax.rem(z, 2), lax.rem(z + 2, 4), 3 - z]
-    fx, fy = x + (1 - c) * (1 - 2 * x), y + c * (1 - 2 * y)
-    sx, sy = x + c * (1 - 2 * x), y + (1 - c) * (1 - 2 * y)
+    halves = (0, 1)
+    half = cols // 2
+    f_at, s_at = [(y, 1 - x), (1 - y, x)], [(1 - y, x), (y, 1 - x)]
 
     def dev(zz, xx, yy, cc):
         return (zz * 2 + xx, yy * 2 + cc)
 
     line = [dev(zs[k], x, y, c) for k in range(4)]
     cross = [dev(zs[k], 1 - x, y, c) for k in range(4)]
-    first, second, sibling = dev(z, fx, fy, c), dev(z, sx, sy, c), dev(z, x, y, 1 - c)
+    firsts = [dev(z, 1 - x, y, c), dev(z, x, 1 - y, c)]
+    seconds = firsts[::-1]
+    sibling = dev(z, x, y, 1 - c)
 
     loads = []
 
@@ -77,21 +80,20 @@
     def row_slice(xx):
         return pl.ds(pl.multiple_of(xx * rows, 32), rows)
 
-    def block(k, yy, xx, cc):
-        return buf.at[k, yy * 2 + cc, row_slice(xx), :]
-
-    load(tok_ref, block(0, y, x, c))
-    for s in range(slots):
-        for j in range(tiles):
-            span = pl.ds(j * 128, 128)
-            load(gate_ref.at[s, :, span], wgu.at[s * tiles + j, :, pl.ds(0, 128)])
-            load(up_ref.at[s, :, span], wgu.at[s * tiles + j, :, pl.ds(128, 128)])
-    for s in range(slots):
-        load(down_ref.at[s], wd.at[pl.ds(s * ff, ff), :])
+    def block(k, at, cc, p=None):
+        span = slice(None) if p is None else pl.ds(p * half, half)
+        return buf.at[k, at[0] * 2 + cc, row_slice(at[1]), span]
+
+    load(tok_ref, block(0, (y, x), c))
+
+    barrier = pltpu.get_barrier_semaphore()
+    peers = line[1:] + cross[1:] + firsts + [sibling]
+    for peer in peers:
+        pl.semaphore_signal(barrier, inc=1, device_id=peer, device_id_type=MESH)
 
     ids = ids_ref[...]
     scores = fix_ref[...].astype(F32)
-    gate_norm = scores / jnp.sum(scores, axis=1, keepdims=True)
+    gate_norm = scores / jnp.sum(scores, axis=0, keepdims=True)
     axis_count = swap_ref.shape[0]
     home = lax.div(ids, slots)
     own_swap = jnp.zeros_like(ids)
@@ -101,18 +103,13 @@
         other_swap = jnp.where(home == j, swap_ref[(j + axis_count // 2) % axis_count], other_swap)
     other = lax.rem(home + axis_count // 2, axis_count)
     source = jnp.where(ids - home * slots == own_swap, other * slots + other_swap, ids)
-    lane = lax.broadcasted_iota(jnp.int32, (rows, 128), 1)
-    table = jnp.zeros((rows, 128), F32)
-    for k in range(ids.shape[1]):
-        table = table + jnp.where(source[:, k : k + 1] == lane, gate_norm[:, k : k + 1], 0.0)
-    table = jnp.concatenate([table, jnp.zeros((128 - rows, 128), F32)], axis=0)
-    wt[0, x] = jnp.transpose(table)[: wt.shape[2]]
-
-    barrier = pltpu.get_barrier_semaphore()
-    peers = line[1:] + cross[1:] + [first, second, sibling]
-    for peer in peers:
-        pl.semaphore_signal(barrier, inc=1, device_id=peer, device_id_type=MESH)
-    pl.semaphore_wait(barrier, len(peers))
+    experts = wt.shape[2]
+    sub = lax.broadcasted_iota(jnp.int32, (experts, rows), 0)
+    table = jnp.zeros((experts, rows), F32)
+    for k in range(ids.shape[0]):
+        table = table + jnp.where(source[k : k + 1, :] == sub, gate_norm[k : k + 1, :], 0.0)
+    wt[0, x] = jnp.zeros((experts, 128), F32)
+    wt[0, x, :, 0:rows] = table
 
     started = []
 
@@ -134,40 +131,55 @@
         remote(target, target, ag_send, ag_recv, i, peer).wait_recv()
 
     def base(k):
-        return 3 + 7 * k
+        return 3 + 13 * k
 
     def a0(k):
         if k > 3:
             return
-        mine = block(k, y, x, c)
+        mine = block(k, (y, x), c)
         if k:
             arrived(k - 1, mine, line[k])
-        gather(base(k), mine, mine, first)
-        gather(base(k) + 1, mine, mine, second)
-        gather(base(k) + 3, mine, mine, sibling)
+        for p in halves:
+            part = block(k, (y, x), c, p)
+            gather(base(k) + 3 * p, part, part, firsts[p])
+        for p in halves:
+            part = block(k, (y, x), c, p)
+            gather(base(k) + 3 * p + 1, part, part, seconds[p])
+        gather(base(k) + 6, mine, mine, sibling)
 
     def a1(k):
         if k > 3:
             return
-        got = block(k, fy, fx, c)
-        arrived(base(k), got, first)
-        gather(base(k) + 2, got, got, second)
-        gather(base(k) + 4, got, got, sibling)
+        for p in halves:
+            got = block(k, f_at[p], c, p)
+            arrived(base(k) + 3 * p, got, firsts[p])
+            gather(base(k) + 3 * p + 2, got, got, seconds[p])
+            gather(base(k) + 7 + p, got, got, sibling)
+
+    def second_blocks(k, cc):
+        return [
+            (2 * p + n, block(k, at, cc, p), seconds[p])
+            for n in (0, 1)
+            for p, at in enumerate(s_at if n == 0 else [(1 - y, 1 - x)] * 2)
+        ]
 
     def a2(k):
         if k > 3:
             return
-        for n, got in enumerate([block(k, sy, sx, c), block(k, 1 - y, 1 - x, c)]):
-            arrived(base(k) + 1 + n, got, second)
-            gather(base(k) + 5 + n, got, got, sibling)
+        for i, got, peer in second_blocks(k, c):
+            arrived(base(k) + 3 * (i // 2) + 1 + i % 2, got, peer)
+            gather(base(k) + 9 + i, got, got, sibling)
 
     def a3(k):
         if k > 3:
             return
-        for n, (yy, xx) in enumerate([(y, x), (sy, sx), (fy, fx), (1 - y, 1 - x)]):
-            arrived(base(k) + 3 + n, block(k, yy, xx, 1 - c), sibling)
-
-    a_me, b_me = y + c * (x - y), x + c * (y - x)
+        arrived(base(k) + 6, block(k, (y, x), 1 - c), sibling)
+        for p in halves:
+            arrived(base(k) + 7 + p, block(k, f_at[p], 1 - c, p), sibling)
+        for i, got, _ in second_blocks(k, 1 - c):
+            arrived(base(k) + 9 + i, got, sibling)
+
+    a_me, b_me = [y, x], [x, y]
 
     def scatter(i, source, target, peer):
         send(source, target, rs_send, rs_recv, i, peer)
@@ -175,42 +187,50 @@
     def summed(i, target, peer):
         remote(target, target, rs_send, rs_recv, i, peer).wait_recv()
 
+    def add(k, p, a, b, other):
+        pbuf[k, c, p, a, b] = (pbuf[k, c, p, a, b].astype(F32) + other.astype(F32)).astype(BF16)
+
     def r0(k):
-        scatter(4 * k, pbuf.at[k, 1 - c], rs_sib.at[k], sibling)
+        scatter(7 * k, pbuf.at[k, 1 - c], rs_sib.at[k], sibling)
 
     def r1(k):
         if k < 0:
             return
-        summed(4 * k, rs_sib.at[k], sibling)
-        away = 1 - a_me
-        pbuf[k, c, away] = (pbuf[k, c, away].astype(F32) + rs_sib[k, away].astype(F32)).astype(BF16)
-        scatter(4 * k + 1, pbuf.at[k, c, away], rs_sec.at[k], second)
-        pbuf[k, c, a_me] = (pbuf[k, c, a_me].astype(F32) + rs_sib[k, a_me].astype(F32)).astype(BF16)
+        summed(7 * k, rs_sib.at[k], sibling)
+        for p in halves:
+            away = 1 - a_me[p]
+            for b in (0, 1):
+                add(k, p, away, b, rs_sib[k, p, away, b])
+            scatter(7 * k + 1 + p, pbuf.at[k, c, p, away], rs_sec.at[k, p], seconds[p])
+        for p in halves:
+            for b in (0, 1):
+                add(k, p, a_me[p], b, rs_sib[k, p, a_me[p], b])
 
     def r2(k):
         if k < 0:
             return
-        summed(4 * k + 1, rs_sec.at[k], second)
-        away = 1 - b_me
-        pbuf[k, c, a_me, away] = (
-            pbuf[k, c, a_me, away].astype(F32) + rs_sec[k, away].astype(F32)
-        ).astype(BF16)
-        scatter(4 * k + 2, pbuf.at[k, c, a_me, away], rs_fst.at[k], first)
+        for p in halves:
+            summed(7 * k + 1 + p, rs_sec.at[k, p], seconds[p])
+            away = 1 - b_me[p]
+            add(k, p, a_me[p], away, rs_sec[k, p, away])
+            scatter(7 * k + 3 + p, pbuf.at[k, c, p, a_me[p], away], rs_fst.at[k, p], firsts[p])
 
     def r3(k):
         if k < 0:
             return
-        summed(4 * k + 2, rs_fst.at[k], first)
-        total = (
-            pbuf[k, c, a_me, b_me].astype(F32)
-            + rs_sec[k, b_me].astype(F32)
-            + rs_fst[k].astype(F32)
-        )
-        if k:
-            pbuf[k, c, a_me, b_me] = total.astype(BF16)
-            scatter(4 * k + 3, pbuf.at[k, c, a_me, b_me], rs_z.at[k - 1], line[k])
-        else:
-            own_sum[...] = total
+        for p in halves:
+            summed(7 * k + 3 + p, rs_fst.at[k, p], firsts[p])
+            total = (
+                pbuf[k, c, p, a_me[p], b_me[p]].astype(F32)
+                + rs_sec[k, p, b_me[p]].astype(F32)
+                + rs_fst[k, p].astype(F32)
+            )
+            if k:
+                pbuf[k, c, p, a_me[p], b_me[p]] = total.astype(BF16)
+                mine = pbuf.at[k, c, p, a_me[p], b_me[p]]
+                scatter(7 * k + 5 + p, mine, rs_z.at[k - 1, p], line[k])
+            else:
+                own_sum[p] = total
 
     def weight_columns(k):
         for xx in range(2):
@@ -239,27 +259,38 @@
             out = jnp.dot(hid[...], wd[:, q * cols : (q + 1) * cols], preferred_element_type=F32)
             out = out.astype(BF16)
             yy, cc = q // 2, q % 2
-            for xx in range(2):
-                a, b = (yy, xx) if cc == 0 else (xx, yy)
-                pbuf[k, cc, a, b] = out[xx * rows : (xx + 1) * rows]
-
+            for p in halves:
+                for xx in range(2):
+                    a, b = (yy, xx) if p == 0 else (xx, yy)
+                    pbuf[k, cc, p, a, b] = out[
+                        xx * rows : (xx + 1) * rows, p * half : (p + 1) * half
+                    ]
+
+    pl.semaphore_wait(barrier, len(peers))
     loads[0].wait()
-    gather_own = block(0, y, x, c)
+    own = block(0, (y, x), c)
     a0(0)
     for k in (1, 2, 3):
-        gather(k - 1, gather_own, block(k, y, x, c), line[k])
+        gather(k - 1, own, block(k, (y, x), c), line[k])
     tags = [(line[1], 1, 0), (line[2], 2, 1), (line[3], 3, 2)]
     tags += [(cross[k], k, 3 + k) for k in range(4)]
     for peer, k, i in tags:
         send(wt.at[0, x], wt.at[k, x], wt_send, wt_recv, i, peer)
+    for s in range(slots):
+        for j in range(tiles):
+            span = pl.ds(j * 128, 128)
+            load(gate_ref.at[s, :, span], wgu.at[s * tiles + j, :, pl.ds(0, 128)])
+            load(up_ref.at[s, :, span], wgu.at[s * tiles + j, :, pl.ds(128, 128)])
+    for s in range(slots):
+        load(down_ref.at[s], wd.at[pl.ds(s * ff, ff), :])
     a1(0)
     a0(1)
     a2(0)
     a1(1)
+    a0(2)
     for peer, k, i in tags:
         got = wt.at[k, x if i < 3 else 1 - x]
         remote(got, got, wt_send, wt_recv, i, peer).wait_recv()
-    a0(2)
     for copy in loads[1:]:
         copy.wait()
     a3(0)
@@ -269,21 +300,23 @@
         a2(k + 1)
         a1(k + 2)
         r1(k - 1)
+        r3(k - 2)
         up_gate(k, 1)
         a0(k + 3)
-        r2(k - 1)
         down(k)
         r0(k)
-        r3(k - 1)
+        r2(k - 1)
         a3(k + 1)
     r1(3)
+    r3(2)
     r2(3)
     r3(3)
-    total = own_sum[...]
-    for k in (1, 2, 3):
-        summed(4 * k + 3, rs_z.at[k - 1], line[k])
-        total = total + rs_z[k - 1].astype(F32)
-    out_ref[...] = total.astype(BF16)
+    for p in halves:
+        total = own_sum[p]
+        for k in (1, 2, 3):
+            summed(7 * k + 5 + p, rs_z.at[k - 1, p], line[k])
+            total = total + rs_z[k - 1, p].astype(F32)
+        out_ref[:, p * half : (p + 1) * half] = total.astype(BF16)
     for copy in started:
         copy.wait_send()
 
@@ -291,7 +324,7 @@
 def fused_device(tokens, gate_weight, up_weight, down_weight, swap_slot, expert_ids, gate_fixed):
     rows, cols = tokens.shape
     slots, width, ff = gate_weight.shape
-    quarters = width // cols
+    quarters, half = width // cols, cols // 2
     chunks = 4
     scratch = [
         pltpu.VMEM((chunks, quarters, 2 * rows, cols), BF16),
@@ -299,20 +332,20 @@
         pltpu.VMEM((slots * ff, width), BF16),
         pltpu.VMEM((2 * rows, slots * ff), BF16),
         pltpu.VMEM((slots, 2 * rows, 128), F32),
-        pltpu.VMEM((chunks, 2, 2, 2, rows, cols), BF16),
+        pltpu.VMEM((chunks, 2, 2, 2, 2, rows, half), BF16),
         pltpu.VMEM((chunks, 2, 16, 128), F32),
-        pltpu.VMEM((chunks, 2, 2, rows, cols), BF16),
-        pltpu.VMEM((chunks, 2, rows, cols), BF16),
-        pltpu.VMEM((chunks, rows, cols), BF16),
-        pltpu.VMEM((chunks - 1, rows, cols), BF16),
-        pltpu.VMEM((rows, cols), F32),
+        pltpu.VMEM((chunks, 2, 2, 2, rows, half), BF16),
+        pltpu.VMEM((chunks, 2, 2, rows, half), BF16),
+        pltpu.VMEM((chunks, 2, rows, half), BF16),
+        pltpu.VMEM((chunks - 1, 2, rows, half), BF16),
+        pltpu.VMEM((2, rows, half), F32),
         pltpu.SemaphoreType.DMA((1 + 2 * slots * (ff // 128) + slots,)),
-        pltpu.SemaphoreType.DMA((3 + 7 * chunks,)),
-        pltpu.SemaphoreType.DMA((3 + 7 * chunks,)),
+        pltpu.SemaphoreType.DMA((3 + 13 * chunks,)),
+        pltpu.SemaphoreType.DMA((3 + 13 * chunks,)),
         pltpu.SemaphoreType.DMA((7,)),
         pltpu.SemaphoreType.DMA((7,)),
-        pltpu.SemaphoreType.DMA((4 * chunks,)),
-        pltpu.SemaphoreType.DMA((4 * chunks,)),
+        pltpu.SemaphoreType.DMA((7 * chunks,)),
+        pltpu.SemaphoreType.DMA((7 * chunks,)),
     ]
     any_space = pl.BlockSpec(memory_space=pl.ANY)
     vmem = pl.BlockSpec(memory_space=pltpu.VMEM)
@@ -325,7 +358,7 @@
         compiler_params=pltpu.CompilerParams(
             collective_id=0, has_side_effects=True, vmem_limit_bytes=56 * 1024 * 1024
         ),
-    )(tokens, gate_weight, up_weight, down_weight, expert_ids, gate_fixed, swap_slot)
+    )(tokens, gate_weight, up_weight, down_weight, expert_ids.T, gate_fixed.T, swap_slot)
 
 
 def per_device(tokens, *rest):

time: 110 us -> 83 us (0.75)
  Pallas kernels: 105 us -> 80.7 us
  local copies, waits for them, and re-layouts: 4.41 us -> 1.62 us
    pallas_call x1, Pallas kernels: 105 us -> 80.7 us  [fused_device(): pl.pallas_call(fused_kernel, out_shape=jax.ShapeDtypeStruct((rows, cols),...]
    unnamed x3 -> x1, local copies, waits for them, and re-layouts: 4.41 us -> 1.62 us
where the time goes in v3:
time: 83 us; the launch traced here: 82.3 us
  Pallas kernels  80.7 us (97%)
  local copies, waits for them, and re-layouts  1.62 us (2%)
    pallas_call x1, Pallas kernels, fused_device(): pl.pallas_call(fused_kernel, out_shape=jax.ShapeDtypeStruct((rows, cols),...  80.7 us

profile of v3, /device:TPU:8, one launch (start us, length us, event | category | flops | bytes accessed | tf_op | source)
XLA Modules:
  0.0 82.3 jit_solution(7682803707820536721)
XLA Ops:
  0.0 80.7 %shard_map.73 = bf16[96,1024]{1,0:T(8,128)(2,1)} custom-call(bf16[96,1024]{1,0:T(8,128)(2,1)} %tok_ref.1, bf16[2,4096,384]{2,1,0:T(8,128)(2,1)} %gate_ref.1, bf16[2,4096,384]{2,1,0:T(8,128)(2,1)} %up_ref.1, bf16[2,384,4096]{2,1,0:T(8,128)(2,1)} %down_ref.1, s32[8,96]{1,0:T(8,128)} %bitcast.2, s32[8,96]{1,0:T(8,128)} %bitcast.3, s32[8]{0:T(128)} %swap_ref.1), custom_call_target="tpu_custom_call" | custom-call | tf_op jit(solution)/shard_map/pallas_call | solution.py:352
  80.7 1.6 %copy.9 = bf16[96,1024]{1,0:T(8,128)(2,1)} copy(bf16[96,1024]{1,0:T(8,128)(2,1)} %shard_map.73) | data formatting | bytes 393216

commit v4 on v3

--- a/solution.py
+++ b/solution.py
@@ -269,9 +269,11 @@
     pl.semaphore_wait(barrier, len(peers))
     loads[0].wait()
     own = block(0, (y, x), c)
+    along = [
+        remote(own, block(k, (y, x), c), ag_send, ag_recv, k - 1, line[k]) for k in (1, 2, 3)
+    ]
+    along[0].start()
     a0(0)
-    for k in (1, 2, 3):
-        gather(k - 1, own, block(k, (y, x), c), line[k])
     tags = [(line[1], 1, 0), (line[2], 2, 1), (line[3], 3, 2)]
     tags += [(cross[k], k, 3 + k) for k in range(4)]
     for peer, k, i in tags:
@@ -284,10 +286,11 @@
     for s in range(slots):
         load(down_ref.at[s], wd.at[pl.ds(s * ff, ff), :])
     a1(0)
+    along[0].wait_send()
+    along[1].start()
     a0(1)
     a2(0)
     a1(1)
-    a0(2)
     for peer, k, i in tags:
         got = wt.at[k, x if i < 3 else 1 - x]
         remote(got, got, wt_send, wt_recv, i, peer).wait_recv()
@@ -297,12 +300,16 @@
     for k in range(4):
         weight_columns(k)
         up_gate(k, 0)
-        a2(k + 1)
-        a1(k + 2)
+        if k == 0:
+            along[1].wait_send()
+            along[2].start()
+            started.append(along[2])
         r1(k - 1)
         r3(k - 2)
+        a2(k + 1)
+        a0(k + 2)
         up_gate(k, 1)
-        a0(k + 3)
+        a1(k + 2)
         down(k)
         r0(k)
         r2(k - 1)

time: 83 us -> 80.6 us (0.971)
  Pallas kernels: 80.7 us -> 78.3 us
    pallas_call x1, Pallas kernels: 80.7 us -> 78.3 us  [fused_device(): pl.pallas_call(fused_kernel, out_shape=jax.ShapeDtypeStruct((rows, cols),...]
where the time goes in v4:
time: 80.6 us; the launch traced here: 79.9 us
  Pallas kernels  78.3 us (97%)
  local copies, waits for them, and re-layouts  1.62 us (2%)
    pallas_call x1, Pallas kernels, fused_device(): pl.pallas_call(fused_kernel, out_shape=jax.ShapeDtypeStruct((rows, cols),...  78.3 us
    unnamed x1, local copies, waits for them, and re-layouts  1.62 us

profile of v4, /device:TPU:8, one launch (start us, length us, event | category | flops | bytes accessed | tf_op | source)
XLA Modules:
  0.0 79.9 jit_solution(3722169204955960872)
XLA Ops:
  0.0 78.3 %shard_map.73 = bf16[96,1024]{1,0:T(8,128)(2,1)} custom-call(bf16[96,1024]{1,0:T(8,128)(2,1)} %tok_ref.1, bf16[2,4096,384]{2,1,0:T(8,128)(2,1)} %gate_ref.1, bf16[2,4096,384]{2,1,0:T(8,128)(2,1)} %up_ref.1, bf16[2,384,4096]{2,1,0:T(8,128)(2,1)} %down_ref.1, s32[8,96]{1,0:T(8,128)} %bitcast.2, s32[8,96]{1,0:T(8,128)} %bitcast.3, s32[8]{0:T(128)} %swap_ref.1), custom_call_target="tpu_custom_call" | custom-call | tf_op jit(solution)/shard_map/pallas_call | solution.py:359
  78.3 1.6 %copy.9 = bf16[96,1024]{1,0:T(8,128)(2,1)} copy(bf16[96,1024]{1,0:T(8,128)(2,1)} %shard_map.73) | data formatting | bytes 393216
